TPU v7x, 512 devices: a whole 4x4x16 slice. The times are simulated.
512 devices in a mesh: pairs: 128 (over x, z, core), rep: 4 (over y).
Axes of the slice: x: 4, y: 4, z: 16, core: 2. Of those that a mesh axis runs over, the one named last changes fastest.
Arguments:
- positions: float32 [3, 2048, 256], P(None, 'pairs'), may hold values from -1 to 1
- facing: float32 [2, 2048, 256], P(None, 'pairs'), may hold values from -3.140625 to 3.140625
- area: float32 [2048, 256], P('pairs'), may hold values from 0.00390625 to 0.03125
- emission: float32 [2048, 8, 256], P('pairs'), may hold values from 0.1 to 2
- reflect: float32 [2048, 8, 256], P('pairs'), may hold values from 0.2 to 0.9
- pair_list: int32 [128, 4, 128, 1, 2], P('pairs', 'rep'), may hold values from -1 to 2047, as said below
Outputs:
- radiosity: float32 [2048, 8, 256], P('pairs')
Inputs may be any that keep to these rules, and one draw needn't show every extreme that they name: `pair_list`: entry [p, r, q, c] is held by the device at pairs index p and rep index r in its slot c toward pairs index q. Its row block lies in p * 16 to (p + 1) * 16 - 1 and its column block in q * 16 to (q + 1) * 16 - 1, or both entries are -1 for an empty slot. Slots toward pairs index 0 are never empty.
All inputs are finite; a program needn't handle non-finite values.
Results may differ from a plain program's by a relative error of at most 0.0003.
Values may be sent and summed in bfloat16 or wider, within the bound.
A program may use at most 64 MiB of HBM per device.

v0:
```python
import functools
import math

import jax
import jax.numpy as jnp
from jax import lax
from jax.experimental import pallas as pl
from jax.experimental.pallas import tpu as pltpu
from jax.sharding import PartitionSpec as P

MESH = pl.DeviceIdType.MESH
VMEM = pl.BlockSpec(memory_space=pltpu.VMEM)
SMEM = pl.BlockSpec(memory_space=pltpu.SMEM)
F32, BF16, I32 = jnp.float32, jnp.bfloat16, jnp.int32

NX, NY, NZ, NC = 4, 4, 16, 2
NS, NT = NX * NC, NZ
ROOT_PI = math.sqrt(math.pi)
SOFTEN = 0.1


def place():
    p = lax.axis_index("pairs")
    return p // (NZ * NC), lax.axis_index("rep"), (p // NC) % NZ, p % NC


def device(x, y, z, c):
    return {"pairs": (x * NZ + z) * NC + c, "rep": y}


def plane_peer(me, i):
    x, y, z, c = me
    return (x + i // (NY * NC)) % NX, (y + (i // NC) % NY) % NY, z, (c + i % NC) % NC


def line_peer(me, d):
    x, y, z, c = me
    return x, y, (z + d) % NZ, c


def greet(me):
    barrier = pltpu.get_barrier_semaphore()

    def plane(i, _):
        pl.semaphore_signal(barrier, inc=1, device_id=device(*plane_peer(me, i)), device_id_type=MESH)
        return 0

    def line(d, _):
        pl.semaphore_signal(barrier, inc=1, device_id=device(*line_peer(me, d)), device_id_type=MESH)
        return 0

    lax.fori_loop(1, NZ, line, 0)
    lax.fori_loop(1, NX * NY * NC, plane, 0)


def met():
    pl.semaphore_wait(pltpu.get_barrier_semaphore(), NX * NY * NC - 1 + NZ - 1)


def remote(src, dst, sems, i, peer):
    return pltpu.make_async_remote_copy(
        src_ref=src,
        dst_ref=dst,
        send_sem=sems.at[0, i],
        recv_sem=sems.at[1, i],
        device_id=device(*peer),
        device_id_type=MESH,
    )


def start_all(first, last, copy):
    def body(i, _):
        copy(i).start()
        return 0

    lax.fori_loop(first, last, body, 0)


def wait_all(first, last, copy):
    def body(i, _):
        copy(i).wait()
        return 0

    lax.fori_loop(first, last, body, 0)


def gather_kernel(pos_ref, facing_ref, area_ref, emission_ref, code_ref,
                  geo_s, geo_t, w_s, w_t, lists_ref,
                  own_geo, own_w, own_code, codes, sem_gt, sem_wt, sem_gs, sem_ws, sem_l):
    me = place()
    x, y, z, c = me
    mine = x * NC + c
    greet(me)
    azimuth, elevation = facing_ref[0], facing_ref[1]
    flat = jnp.cos(elevation)
    parts = [pos_ref[0], pos_ref[1], pos_ref[2],
             jnp.cos(azimuth) * flat, jnp.sin(azimuth) * flat, jnp.sin(elevation)]
    for k in range(4):
        for comp in range(6):
            own_geo[k, comp * 4 : comp * 4 + 4, :] = parts[comp][4 * k : 4 * k + 4, :]
        own_w[k] = jnp.concatenate(
            [area_ref[4 * k + b : 4 * k + b + 1, :] * emission_ref[4 * k + b] for b in range(4)], axis=0
        ).astype(BF16)
    own_code[...] = code_ref[...]
    met()

    def geo_line(d):
        return remote(own_geo.at[y], geo_t.at[z], sem_gt, d, line_peer(me, d))

    def w_line(d):
        return remote(own_w.at[y], w_t.at[z], sem_wt, d, line_peer(me, d))

    def near_peer(i):
        return (x + i // NC) % NX, y, z, (c + i % NC) % NC

    def geo_plane(i):
        return remote(own_geo, geo_s.at[pl.ds(4 * mine, 4)], sem_gs, i, near_peer(i))

    def w_plane(i):
        return remote(own_w, w_s.at[pl.ds(4 * mine, 4)], sem_ws, i, near_peer(i))

    def list_plane(i):
        return remote(own_code, codes.at[mine * NY + y], sem_l, i, plane_peer(me, i))

    start_all(1, NZ, geo_line)
    start_all(1, NZ, w_line)
    start_all(1, NX * NY * NC, list_plane)
    start_all(1, NS, geo_plane)
    start_all(1, NS, w_plane)
    geo_t[z] = own_geo[y]
    w_t[z] = own_w[y]
    geo_s[pl.ds(4 * mine, 4)] = own_geo[...]
    w_s[pl.ds(4 * mine, 4)] = own_w[...]
    codes[mine * NY + y] = own_code[...]
    wait_all(1, NX * NY * NC, list_plane)
    for s in range(NX * NY * NC):
        lists_ref[s : s + 1, :] = codes[s, 0:1, :]
    code = lists_ref[...]
    lane = lax.broadcasted_iota(I32, code.shape, 1)
    owner = lax.broadcasted_iota(I32, code.shape, 0) >> 2
    ours = (code >= 0) & ((lane >> 5) == x) & ((lane & 1) == c) & (((code >> 2) & 3) == y)
    entry = (owner * 16 + (code >> 4)) | (((((lane & 31) >> 1) * 4) + (code & 3)) << 8)
    lists_ref[...] = jnp.where(ours, entry, -1)
    wait_all(1, NS, geo_plane)
    wait_all(1, NS, w_plane)
    wait_all(1, NZ, geo_line)
    wait_all(1, NZ, w_line)


def three(v):
    high = v.astype(BF16)
    rest = v - high.astype(F32)
    middle = rest.astype(BF16)
    return high, middle, (rest - middle.astype(F32)).astype(BF16)


PAIRS_KEPT = 128
RING = 4
UNUSED = (16 * NS) | ((4 * NT) << 8)


def unpack_geometry(q, geo, g, spread_geo):
    data = geo[q]
    product = data[0:12] * data[12:24]
    square = data[0:12] * data[0:12]
    product = product[0:4] + product[4:8] + product[8:12]
    square = square[0:4] + square[4:8] + square[8:12]
    for half in range(2):
        lanes = slice(128 * half, 128 * half + 128)
        spread_geo[half, 0:24, :] = data[:, lanes]
        spread_geo[half, 24:28, :] = product[:, lanes]
        spread_geo[half, 28:32, :] = square[:, lanes]
        for b in range(4):
            g[4 * q + b, :, lanes] = spread_geo[half, pl.ds(b, 8, stride=4), :]


def unpack_values(q, w, v):
    values = w[q].astype(F32)
    for b in range(4):
        v[4 * q + b] = values[8 * b : 8 * b + 8]


def clear_tail(*refs):
    for ref in refs:
        ref[ref.shape[0] - 1] = jnp.zeros((8, 256), F32)


def couple(entry, g_s, g_t):
    gi, gj = g_s[entry & 255], g_t[entry >> 8]
    row = lax.broadcasted_iota(I32, (8, 256), 0)
    unit = jnp.where(row == 0, 1.0, 0.0).astype(F32)
    zero = jnp.zeros((8, 256), F32)
    h, m, l = three(jnp.concatenate([gi, unit], axis=0))
    left = jnp.concatenate([h, h, m, h, l, m], axis=0).T
    near = jnp.where((row >= 3) & (row < 6), pltpu.roll(gj, 3, 0), jnp.where(row == 6, -1.0, 0.0))
    far = jnp.where(row < 3, pltpu.roll(gj, 5, 0), 0.0)
    far_low = jnp.where(row == 0, -pltpu.roll(gj, 2, 0), 0.0)
    dist = jnp.where(row < 3, (-2.0 * ROOT_PI) * gj, jnp.where(row == 7, ROOT_PI, 0.0))
    dist_low = jnp.where(row == 0, ROOT_PI * (pltpu.roll(gj, 1, 0) + SOFTEN), 0.0)
    outs = []
    for top, low in ((near, zero), (far, far_low), (dist, dist_low)):
        h, m, l = three(jnp.concatenate([top, low], axis=0))
        right = jnp.concatenate([h, m, h, l, h, m], axis=0)
        outs.append(jnp.dot(left, right, preferred_element_type=F32))
    near, far, dist = outs
    inverse = pl.reciprocal(dist, approx=False)
    return (jnp.maximum(near, 0.0) * jnp.maximum(far, 0.0) * (inverse * inverse)).astype(BF16)


def apply(entry, kernel, v_s, v_t, acc_s, acc_t):
    i, j = entry & 255, entry >> 8
    acc_s[i & (16 * NS - 1)] += lax.dot_general(
        v_t[j].astype(BF16), kernel, (((1,), (1,)), ((), ())), preferred_element_type=F32
    )
    acc_t[j & (4 * NT - 1)] += jnp.dot(v_s[i].astype(BF16), kernel, preferred_element_type=F32)


def pair_kernel(lists_ref, geo_s, geo_t, w_s, w_t, acc_s, acc_t, order, cache,
                g_s, g_t, v_s, v_t, spread_geo, held, sem):
    x, y, z, c = place()
    acc_s[...] = jnp.zeros_like(acc_s)
    acc_t[...] = jnp.zeros_like(acc_t)
    held[...] = jnp.zeros_like(held)
    clear_tail(g_s, g_t, v_s, v_t)
    base = x * (NZ * NC) + c

    def prepare_t(q, _):
        unpack_geometry(q, geo_t, g_t, spread_geo)
        unpack_values(q, w_t, v_t)
        return 0

    def prepare_s(q, count):
        unpack_geometry(q, geo_s, g_s, spread_geo)
        unpack_values(q, w_s, v_s)
        for zz in range(NZ):
            entry = lists_ref[q, base + zz * NC]
            order[count] = entry
            count = count + 1 + (entry >> 31)
        return count

    lax.fori_loop(0, NT, prepare_t, 0)
    count = lax.fori_loop(0, 4 * NS, prepare_s, jnp.int32(1))
    order[count] = jnp.int32(UNUSED)
    order[0] = count - 1
    turns = count >> 1

    def keep(u):
        return pltpu.make_async_copy(held.at[u & (RING - 1)], cache.at[u], sem.at[u & (RING - 1)])

    def turn(t, last):
        @pl.when((t >= 1) & (t <= PAIRS_KEPT))
        def _():
            keep(t - 1).start()

        @pl.when((t >= RING) & (t < PAIRS_KEPT + RING))
        def _():
            keep(t - RING).wait()

        now = (order[2 * t + 1], order[2 * t + 2])
        for k in range(2):
            apply(last[k], held[(t + RING - 1) & (RING - 1), k], v_s, v_t, acc_s, acc_t)
        for k in range(2):
            held[t & (RING - 1), k] = couple(now[k], g_s, g_t)
        return now

    nothing = (jnp.int32(UNUSED), jnp.int32(UNUSED))
    last = lax.fori_loop(0, turns, turn, nothing)

    @pl.when((turns >= 1) & (turns <= PAIRS_KEPT))
    def _():
        keep(turns - 1).start()

    for k in range(2):
        apply(last[k], held[(turns + RING - 1) & (RING - 1), k], v_s, v_t, acc_s, acc_t)

    def drain(u, _):
        keep(u).wait()
        return 0

    lax.fori_loop(jnp.maximum(turns - RING, 0), jnp.minimum(turns, PAIRS_KEPT), drain, 0)


DEPTH = 8


def again_kernel(order, geo_s, geo_t, w_s, w_t, cache, acc_s, acc_t,
                 g_s, g_t, v_s, v_t, spread_geo, held, sem):
    turns = (order[0] + 1) >> 1
    kept = jnp.minimum(turns, PAIRS_KEPT)

    def fetch(u):
        return pltpu.make_async_copy(cache.at[u], held.at[u & (DEPTH - 1)], sem.at[u & (DEPTH - 1)])

    def begin(u, _):
        fetch(u).start()
        return 0

    lax.fori_loop(0, jnp.minimum(kept, DEPTH), begin, 0)
    acc_s[...] = jnp.zeros_like(acc_s)
    acc_t[...] = jnp.zeros_like(acc_t)
    clear_tail(g_s, g_t, v_s, v_t)

    def prepare_s(q, _):
        unpack_values(q, w_s, v_s)
        return 0

    def prepare_t(q, _):
        unpack_values(q, w_t, v_t)
        return 0

    lax.fori_loop(0, 4 * NS, prepare_s, 0)
    lax.fori_loop(0, NT, prepare_t, 0)

    def turn(t, _):
        fetch(t).wait()
        for k in range(2):
            apply(order[2 * t + 1 + k], held[t & (DEPTH - 1), k], v_s, v_t, acc_s, acc_t)

        @pl.when(t + DEPTH < kept)
        def _():
            fetch(t + DEPTH).start()

        return 0

    lax.fori_loop(0, kept, turn, 0)

    @pl.when(turns > PAIRS_KEPT)
    def _():
        def shape_s(q, _):
            unpack_geometry(q, geo_s, g_s, spread_geo)
            return 0

        def shape_t(q, _):
            unpack_geometry(q, geo_t, g_t, spread_geo)
            return 0

        def more(t, _):
            entry = order[t]
            apply(entry, couple(entry, g_s, g_t), v_s, v_t, acc_s, acc_t)
            return 0

        lax.fori_loop(0, 4 * NS, shape_s, 0)
        lax.fori_loop(0, NT, shape_t, 0)
        lax.fori_loop(2 * PAIRS_KEPT + 1, 2 * turns + 1, more, 0)


def reduce_parts(me, acc_s, acc_t, got_s, got_t, sem_s, sem_t):
    x, y, z, c = me

    def line(d):
        peer = line_peer(me, d)
        return remote(acc_t.at[peer[2]], got_t.at[d], sem_t, d, peer)

    def plane(i):
        peer = plane_peer(me, i)
        return remote(acc_s.at[(peer[0] * NC + peer[3]) * 4 + peer[1]], got_s.at[i], sem_s, i, peer)

    start_all(1, NZ, line)
    start_all(1, NX * NY * NC, plane)
    wait_all(1, NX * NY * NC, plane)
    total = acc_s[(x * NC + c) * 4 + y] + acc_t[z]
    total = lax.fori_loop(1, NX * NY * NC, lambda i, t: t + got_s[i], total)
    wait_all(1, NZ, line)
    return lax.fori_loop(1, NZ, lambda d, t: t + got_t[d], total)


def turn_kernel(acc_s, acc_t, area_ref, emission_ref, reflect_ref, w_s, w_t,
                got_s, got_t, own_w, sem_s, sem_t, sem_ws, sem_wt):
    me = place()
    x, y, z, c = me
    greet(me)
    met()
    total = reduce_parts(me, acc_s, acc_t, got_s, got_t, sem_s, sem_t)
    radiosity = emission_ref[y] + reflect_ref[y] * total
    area = jnp.concatenate(
        [jnp.broadcast_to(area_ref[pl.ds(4 * y + b, 1), :], (8, 256)) for b in range(4)], axis=0
    )
    own_w[...] = (area * radiosity).astype(BF16)
    slot = (x * NC + c) * 4 + y

    def line(d):
        return remote(own_w, w_t.at[z], sem_wt, d, line_peer(me, d))

    def plane(i):
        return remote(own_w, w_s.at[slot], sem_ws, i, plane_peer(me, i))

    start_all(1, NZ, line)
    start_all(1, NX * NY * NC, plane)
    w_t[z] = own_w[...]
    w_s[slot] = own_w[...]
    wait_all(1, NX * NY * NC, plane)
    wait_all(1, NZ, line)


def last_kernel(acc_s, acc_t, emission_ref, reflect_ref, out_ref,
                got_s, got_t, own, sem_s, sem_t, sem_o):
    me = place()
    x, y, z, c = me
    greet(me)
    met()
    total = reduce_parts(me, acc_s, acc_t, got_s, got_t, sem_s, sem_t)
    own[...] = emission_ref[y] + reflect_ref[y] * total

    def across(i):
        return remote(own, out_ref.at[y], sem_o, i, (x, (y + i) % NY, z, c))

    start_all(1, NY, across)
    out_ref[y] = own[...]
    wait_all(1, NY, across)


def sems(n):
    return pltpu.SemaphoreType.DMA((2, n))


def shape(dims, dtype=F32):
    return jax.ShapeDtypeStruct(dims, dtype)


def call(kernel, ident, inputs, outputs, scratch, name, specs=None, out_specs=None):
    params = {"vmem_limit_bytes": 60 * 1024 * 1024}
    if ident is not None:
        params.update(collective_id=ident, has_side_effects=True)
    return pl.pallas_call(
        kernel,
        out_shape=outputs,
        in_specs=specs or [VMEM] * len(inputs),
        out_specs=out_specs or [VMEM] * len(outputs),
        scratch_shapes=scratch,
        compiler_params=pltpu.CompilerParams(**params),
        name=name,
    )(*inputs)


ANY = pl.BlockSpec(memory_space=pl.ANY)


def pairs_call(first, lists, geo_s, geo_t, w_s, w_t, cache=None):
    outputs = [shape((16 * NS, 8, 256)), shape((4 * NT, 8, 256))]
    scratch = [pltpu.VMEM((16 * NS + 1, 8, 256), F32), pltpu.VMEM((4 * NT + 1, 8, 256), F32),
               pltpu.VMEM((16 * NS + 1, 8, 256), F32), pltpu.VMEM((4 * NT + 1, 8, 256), F32),
               pltpu.VMEM((2, 32, 128), F32)]
    depth = RING if first else DEPTH
    scratch += [pltpu.VMEM((depth, 2, 256, 256), BF16), pltpu.SemaphoreType.DMA((depth,))]
    if first:
        outputs += [shape((544,), I32), shape((PAIRS_KEPT, 2, 256, 256), BF16)]
        acc_s, acc_t, order, cache = call(
            pair_kernel, None, (lists, geo_s, geo_t, w_s, w_t), outputs, scratch, "pairs",
            [SMEM] + [VMEM] * 4, [VMEM, VMEM, SMEM, ANY],
        )
    else:
        acc_s, acc_t = call(
            again_kernel, None, (lists, geo_s, geo_t, w_s, w_t, cache), outputs, scratch, "again",
            [SMEM] + [VMEM] * 4 + [ANY],
        )
        order = lists
    return acc_s.reshape(4 * NS, 32, 256), acc_t.reshape(NT, 32, 256), order, cache


def shards(positions, facing, area, emission, reflect, pair_list):
    held = pair_list.reshape(128, 2)
    code = jnp.where(held[:, 0] >= 0, (held[:, 0] % 16) * 16 + held[:, 1] % 16, -1)
    code = jnp.broadcast_to(code[None, :], (8, 128))
    plane = NX * NY * NC
    geo_s, geo_t, w_s, w_t, lists = call(
        gather_kernel, 0, (positions, facing, area, emission, code),
        [shape((4 * NS, 24, 256)), shape((NT, 24, 256)), shape((4 * NS, 32, 256), BF16),
         shape((NT, 32, 256), BF16), shape((plane, 128), I32)],
        [pltpu.VMEM((4, 24, 256), F32), pltpu.VMEM((4, 32, 256), BF16), pltpu.VMEM((8, 128), I32),
         pltpu.VMEM((plane, 8, 128), I32), sems(NZ), sems(NZ), sems(NS), sems(NS), sems(plane)],
        "gather",
    )

    emission4, reflect4 = emission.reshape(4, 32, 256), reflect.reshape(4, 32, 256)
    landing = [pltpu.VMEM((plane, 32, 256), F32), pltpu.VMEM((NZ, 32, 256), F32)]
    acc_s, acc_t, order, cache = pairs_call(True, lists, geo_s, geo_t, w_s, w_t)
    w_s, w_t = call(
        turn_kernel, 1, (acc_s, acc_t, area, emission4, reflect4),
        [shape((4 * NS, 32, 256), BF16), shape((NT, 32, 256), BF16)],
        landing + [pltpu.VMEM((32, 256), BF16), sems(plane), sems(NZ), sems(plane), sems(NZ)],
        "turn",
    )
    acc_s, acc_t, _, _ = pairs_call(False, order, geo_s, geo_t, w_s, w_t, cache)
    (out,) = call(
        last_kernel, 2, (acc_s, acc_t, emission4, reflect4), [shape((4, 32, 256))],
        landing + [pltpu.VMEM((32, 256), F32), sems(plane), sems(NZ), sems(NY)],
        "last",
    )
    return out.reshape(16, 8, 256)


def solution(mesh):
    placed = (
        P(None, "pairs", None),
        P(None, "pairs", None),
        P("pairs", None),
        P("pairs", None, None),
        P("pairs", None, None),
        P("pairs", "rep", None, None, None),
    )
    return jax.shard_map(
        shards, mesh=mesh, in_specs=placed, out_specs=P("pairs", None, None), check_vma=False
    )
```

profile of v0, /device:TPU:6, one launch (start us, length us, event | category | flops | bytes accessed | tf_op | source)
XLA Modules:
  0.0 179.8 jit_solution(9366487550122739400)
XLA Ops:
  0.0 0.8 compare_select_fusion.4
  0.8 0.6 broadcast_in_dim.11.code_ref
  1.4 51.3 %gather.1 = (f32[32,24,256]{2,1,0:T(8,128)}, f32[16,24,256]{2,1,0:T(8,128)}, bf16[32,32,256]{2,1,0:T(8,128)(2,1)}, bf16[16,32,256]{2,1,0:T(8,128)(2,1)}, s32[32,128]{1,0:T(8,128)}) custom-call(f32[3,16,256]{2,1,0:T(8,128)} %pos_ref.1, f32[2,16,256]{2,1,0:T(8,128)} %facing_ref.1, f32[16,256]{1,0:T(8,128)} %area_ref.3, f32[16,8,256]{2,1,0:T(8,128)} %emission_ref.1, ...), custom_call_target="tpu_custom_call" | custom-call | tf_op jit(solution)/shard_map/gather/pallas_call | solution.py:424
  52.6 20.5 %pairs.1 = (f32[128,8,256]{2,1,0:T(8,128)}, f32[64,8,256]{2,1,0:T(8,128)}, s32[544]{0:T(1024)}, bf16[128,2,256,256]{3,2,1,0:T(8,128)(2,1)}) custom-call(s32[32,128]{1,0:T(8,128)} %get-tuple-element.18.lists_ref, f32[32,24,256]{2,1,0:T(8,128)} %get-tuple-element.19.geo_s, f32[16,24,256]{2,1,0:T(8,128)} %get-tuple-element.20.geo_t, ...), custom_call_target="tpu_custom_call" | custom-call | tf_op jit(solution)/shard_map/pairs/pallas_call | solution.py:424
  73.1 48.8 %turn.1 = (bf16[32,32,256]{2,1,0:T(8,128)(2,1)}, bf16[16,32,256]{2,1,0:T(8,128)(2,1)}) custom-call(f32[32,32,256]{2,1,0:T(8,128)} %bitcast.14, f32[16,32,256]{2,1,0:T(8,128)} %bitcast.16, f32[16,256]{1,0:T(8,128)} %area_ref.3, f32[4,32,256]{2,1,0:T(8,128)} %bitcast.12, f32[4,32,256]{2,1,0:T(8,128)} %bitcast.17), custom_call_target="tpu_custom_call" | custom-call | tf_op jit(solution)/shard_map/turn/pallas_call | solution.py:424
  122.0 10.8 %again.1 = (f32[128,8,256]{2,1,0:T(8,128)}, f32[64,8,256]{2,1,0:T(8,128)}) custom-call(s32[544]{0:T(1024)} %get-tuple-element.23.order, f32[32,24,256]{2,1,0:T(8,128)} %get-tuple-element.19.geo_s, f32[16,24,256]{2,1,0:T(8,128)} %get-tuple-element.20.geo_t, bf16[32,32,256]{2,1,0:T(8,128)(2,1)} %get-tuple-element.26.w_s, ...), custom_call_target="tpu_custom_call" | custom-call | tf_op jit(solution)/shard_map/again/pallas_call | solution.py:424
  132.8 45.4 %last.1 = f32[4,32,256]{2,1,0:T(8,128)} custom-call(f32[32,32,256]{2,1,0:T(8,128)} %bitcast.15, f32[16,32,256]{2,1,0:T(8,128)} %bitcast.19, f32[4,32,256]{2,1,0:T(8,128)} %bitcast.13, f32[4,32,256]{2,1,0:T(8,128)} %bitcast.18), custom_call_target="tpu_custom_call" | custom-call | tf_op jit(solution)/shard_map/last/pallas_call | solution.py:424
  178.2 1.6 copy.8
where the time goes:
time: 179 us; the launch traced here: 180 us
  Pallas kernels  177 us (99%)
  local copies, waits for them, and re-layouts  2.16 us (1%)
    pallas_call x5, Pallas kernels, call(): pl.pallas_call(kernel, out_shape=outputs, in_specs=specs or [VMEM] * len(...  177 us

commit v1 on v0

--- a/solution.py
+++ b/solution.py
@@ -35,26 +35,28 @@
 
 def line_peer(me, d):
     x, y, z, c = me
-    return x, y, (z + d) % NZ, c
+    return x, y, (z + d + NZ) % NZ, c
+
+
+FAR = (6, -6, 3, -3)
+NEAR = (1, -1)
+LINE = (1, -1, 2, -2, 3, -3, 6, -6)
 
 
 def greet(me):
     barrier = pltpu.get_barrier_semaphore()
+    for d in LINE:
+        pl.semaphore_signal(barrier, inc=1, device_id=device(*line_peer(me, d)), device_id_type=MESH)
 
     def plane(i, _):
         pl.semaphore_signal(barrier, inc=1, device_id=device(*plane_peer(me, i)), device_id_type=MESH)
         return 0
 
-    def line(d, _):
-        pl.semaphore_signal(barrier, inc=1, device_id=device(*line_peer(me, d)), device_id_type=MESH)
-        return 0
-
-    lax.fori_loop(1, NZ, line, 0)
     lax.fori_loop(1, NX * NY * NC, plane, 0)
 
 
 def met():
-    pl.semaphore_wait(pltpu.get_barrier_semaphore(), NX * NY * NC - 1 + NZ - 1)
+    pl.semaphore_wait(pltpu.get_barrier_semaphore(), NX * NY * NC - 1 + len(LINE))
 
 
 def remote(src, dst, sems, i, peer):
@@ -82,6 +84,35 @@
         return 0
 
     lax.fori_loop(first, last, body, 0)
+
+
+def line_gather(me, own, into, sems):
+    z = me[2]
+    first = [remote(own, into.at[z], sems, n, line_peer(me, h)) for n, h in enumerate(FAR + NEAR)]
+    for copy in first:
+        copy.start()
+
+    def finish():
+        copies = []
+        for n, h in enumerate(FAR):
+            first[n].wait_recv()
+            source = (z - h + NZ) % NZ
+            steps = NEAR + (-2,) if h == -6 else NEAR
+            for k, e in enumerate(steps):
+                copy = remote(into.at[source], into.at[source], sems, 6 + 3 * n + k, line_peer(me, e))
+                copy.start()
+                copies.append(copy)
+        first[4].wait_recv()
+        first[5].wait_recv()
+        for copy in copies:
+            copy.wait_recv()
+        for copy in first + copies:
+            copy.wait_send()
+
+    return finish
+
+
+LINE_GATHER = 18
 
 
 def gather_kernel(pos_ref, facing_ref, area_ref, emission_ref, code_ref,
@@ -104,34 +135,33 @@
     own_code[...] = code_ref[...]
     met()
 
-    def geo_line(d):
-        return remote(own_geo.at[y], geo_t.at[z], sem_gt, d, line_peer(me, d))
-
-    def w_line(d):
-        return remote(own_w.at[y], w_t.at[z], sem_wt, d, line_peer(me, d))
-
-    def near_peer(i):
-        return (x + i // NC) % NX, y, z, (c + i % NC) % NC
-
-    def geo_plane(i):
-        return remote(own_geo, geo_s.at[pl.ds(4 * mine, 4)], sem_gs, i, near_peer(i))
-
-    def w_plane(i):
-        return remote(own_w, w_s.at[pl.ds(4 * mine, 4)], sem_ws, i, near_peer(i))
+    def across(own, into, sems, dx):
+        return remote(own, into.at[pl.ds(4 * mine, 4)], sems, dx, ((x + dx) % NX, y, z, c))
+
+    def beside(own, into, sems, dx):
+        there = pl.ds(4 * (((x - dx + NX) % NX) * NC + c), 4)
+        source = own if dx == 0 else into.at[there]
+        return remote(source, into.at[there], sems, NX + dx, (x, y, z, 1 - c))
 
     def list_plane(i):
         return remote(own_code, codes.at[mine * NY + y], sem_l, i, plane_peer(me, i))
 
-    start_all(1, NZ, geo_line)
-    start_all(1, NZ, w_line)
+    plane = ((own_geo, geo_s, sem_gs), (own_w, w_s, sem_ws))
+    line = (line_gather(me, own_geo.at[y], geo_t, sem_gt), line_gather(me, own_w.at[y], w_t, sem_wt))
+    crossing = [across(*args, dx) for args in plane for dx in range(1, NX)]
+    siblings = [beside(*args, dx) for args in plane for dx in range(NX)]
+    for copy in crossing + [siblings[0], siblings[NX]]:
+        copy.start()
     start_all(1, NX * NY * NC, list_plane)
-    start_all(1, NS, geo_plane)
-    start_all(1, NS, w_plane)
     geo_t[z] = own_geo[y]
     w_t[z] = own_w[y]
     geo_s[pl.ds(4 * mine, 4)] = own_geo[...]
     w_s[pl.ds(4 * mine, 4)] = own_w[...]
     codes[mine * NY + y] = own_code[...]
+    for n in range(2):
+        for dx in range(1, NX):
+            crossing[n * (NX - 1) + dx - 1].wait_recv()
+            siblings[n * NX + dx].start()
     wait_all(1, NX * NY * NC, list_plane)
     for s in range(NX * NY * NC):
         lists_ref[s : s + 1, :] = codes[s, 0:1, :]
@@ -141,10 +171,12 @@
     ours = (code >= 0) & ((lane >> 5) == x) & ((lane & 1) == c) & (((code >> 2) & 3) == y)
     entry = (owner * 16 + (code >> 4)) | (((((lane & 31) >> 1) * 4) + (code & 3)) << 8)
     lists_ref[...] = jnp.where(ours, entry, -1)
-    wait_all(1, NS, geo_plane)
-    wait_all(1, NS, w_plane)
-    wait_all(1, NZ, geo_line)
-    wait_all(1, NZ, w_line)
+    for finish in line:
+        finish()
+    for copy in crossing:
+        copy.wait_send()
+    for copy in siblings:
+        copy.wait()
 
 
 def three(v):
@@ -344,33 +376,58 @@
         lax.fori_loop(2 * PAIRS_KEPT + 1, 2 * turns + 1, more, 0)
 
 
-def reduce_parts(me, acc_s, acc_t, got_s, got_t, sem_s, sem_t):
+def reduce_parts(me, acc_s, acc_t, got_s, got_t, sum_t, far_t, sem_s, sem_t):
     x, y, z, c = me
-
-    def line(d):
-        peer = line_peer(me, d)
-        return remote(acc_t.at[peer[2]], got_t.at[d], sem_t, d, peer)
 
     def plane(i):
         peer = plane_peer(me, i)
         return remote(acc_s.at[(peer[0] * NC + peer[3]) * 4 + peer[1]], got_s.at[i], sem_s, i, peer)
 
-    start_all(1, NZ, line)
+    def toward(n, h, k, e):
+        piece = acc_t.at[(z + e - h + NZ) % NZ]
+        return remote(piece, got_t.at[3 * n + k], sem_t, 3 * n + k, line_peer(me, e))
+
+    hubs = FAR + (0,)
+    near = [[toward(n, h, k, e) for k, e in enumerate(NEAR + (2,) if h == -6 else NEAR)]
+            for n, h in enumerate(hubs)]
+    for copies in near:
+        for copy in copies:
+            copy.start()
     start_all(1, NX * NY * NC, plane)
+    far = []
+    for n, h in enumerate(hubs):
+        part = acc_t[(z - h + NZ) % NZ]
+        for k, copy in enumerate(near[n]):
+            copy.wait_recv()
+            part = part + got_t[3 * n + k]
+        if h:
+            sum_t[n] = part
+            far.append(remote(sum_t.at[n], far_t.at[n], sem_t, 15 + n, line_peer(me, -h)))
+            far[n].start()
+    total = part + acc_s[(x * NC + c) * 4 + y]
     wait_all(1, NX * NY * NC, plane)
-    total = acc_s[(x * NC + c) * 4 + y] + acc_t[z]
     total = lax.fori_loop(1, NX * NY * NC, lambda i, t: t + got_s[i], total)
-    wait_all(1, NZ, line)
-    return lax.fori_loop(1, NZ, lambda d, t: t + got_t[d], total)
+    for n, copy in enumerate(far):
+        copy.wait_recv()
+        total = total + far_t[n]
+    for copies in near:
+        for copy in copies:
+            copy.wait_send()
+    for copy in far:
+        copy.wait_send()
+    return total
+
+
+LINE_SUM = 19
 
 
 def turn_kernel(acc_s, acc_t, area_ref, emission_ref, reflect_ref, w_s, w_t,
-                got_s, got_t, own_w, sem_s, sem_t, sem_ws, sem_wt):
+                got_s, got_t, sum_t, far_t, own_w, sem_s, sem_t, sem_ws, sem_wt):
     me = place()
     x, y, z, c = me
     greet(me)
     met()
-    total = reduce_parts(me, acc_s, acc_t, got_s, got_t, sem_s, sem_t)
+    total = reduce_parts(me, acc_s, acc_t, got_s, got_t, sum_t, far_t, sem_s, sem_t)
     radiosity = emission_ref[y] + reflect_ref[y] * total
     area = jnp.concatenate(
         [jnp.broadcast_to(area_ref[pl.ds(4 * y + b, 1), :], (8, 256)) for b in range(4)], axis=0
@@ -378,27 +435,24 @@
     own_w[...] = (area * radiosity).astype(BF16)
     slot = (x * NC + c) * 4 + y
 
-    def line(d):
-        return remote(own_w, w_t.at[z], sem_wt, d, line_peer(me, d))
-
     def plane(i):
         return remote(own_w, w_s.at[slot], sem_ws, i, plane_peer(me, i))
 
-    start_all(1, NZ, line)
+    finish = line_gather(me, own_w, w_t, sem_wt)
     start_all(1, NX * NY * NC, plane)
     w_t[z] = own_w[...]
     w_s[slot] = own_w[...]
+    finish()
     wait_all(1, NX * NY * NC, plane)
-    wait_all(1, NZ, line)
 
 
 def last_kernel(acc_s, acc_t, emission_ref, reflect_ref, out_ref,
-                got_s, got_t, own, sem_s, sem_t, sem_o):
+                got_s, got_t, sum_t, far_t, own, sem_s, sem_t, sem_o):
     me = place()
     x, y, z, c = me
     greet(me)
     met()
-    total = reduce_parts(me, acc_s, acc_t, got_s, got_t, sem_s, sem_t)
+    total = reduce_parts(me, acc_s, acc_t, got_s, got_t, sum_t, far_t, sem_s, sem_t)
     own[...] = emission_ref[y] + reflect_ref[y] * total
 
     def across(i):
@@ -467,23 +521,24 @@
         [shape((4 * NS, 24, 256)), shape((NT, 24, 256)), shape((4 * NS, 32, 256), BF16),
          shape((NT, 32, 256), BF16), shape((plane, 128), I32)],
         [pltpu.VMEM((4, 24, 256), F32), pltpu.VMEM((4, 32, 256), BF16), pltpu.VMEM((8, 128), I32),
-         pltpu.VMEM((plane, 8, 128), I32), sems(NZ), sems(NZ), sems(NS), sems(NS), sems(plane)],
+         pltpu.VMEM((plane, 8, 128), I32), sems(LINE_GATHER), sems(LINE_GATHER), sems(NS), sems(NS), sems(plane)],
         "gather",
     )
 
     emission4, reflect4 = emission.reshape(4, 32, 256), reflect.reshape(4, 32, 256)
-    landing = [pltpu.VMEM((plane, 32, 256), F32), pltpu.VMEM((NZ, 32, 256), F32)]
+    landing = [pltpu.VMEM((plane, 32, 256), F32), pltpu.VMEM((15, 32, 256), F32),
+               pltpu.VMEM((4, 32, 256), F32), pltpu.VMEM((4, 32, 256), F32)]
     acc_s, acc_t, order, cache = pairs_call(True, lists, geo_s, geo_t, w_s, w_t)
     w_s, w_t = call(
         turn_kernel, 1, (acc_s, acc_t, area, emission4, reflect4),
         [shape((4 * NS, 32, 256), BF16), shape((NT, 32, 256), BF16)],
-        landing + [pltpu.VMEM((32, 256), BF16), sems(plane), sems(NZ), sems(plane), sems(NZ)],
+        landing + [pltpu.VMEM((32, 256), BF16), sems(plane), sems(LINE_SUM), sems(plane), sems(LINE_GATHER)],
         "turn",
     )
     acc_s, acc_t, _, _ = pairs_call(False, order, geo_s, geo_t, w_s, w_t, cache)
     (out,) = call(
         last_kernel, 2, (acc_s, acc_t, emission4, reflect4), [shape((4, 32, 256))],
-        landing + [pltpu.VMEM((32, 256), F32), sems(plane), sems(NZ), sems(NY)],
+        landing + [pltpu.VMEM((32, 256), F32), sems(plane), sems(LINE_SUM), sems(NY)],
         "last",
     )
     return out.reshape(16, 8, 256)

time: 179 us -> 141 us (0.79); the launches traced: 180 us -> 139 us
  Pallas kernels: 177 us -> 136 us
    pallas_call x5, Pallas kernels: 177 us -> 136 us  [call(): pl.pallas_call(kernel, out_shape=outputs, in_specs=specs or [VMEM] * len(...]
where the time goes in v1:
time: 141 us; the launch traced here: 139 us
  Pallas kernels  136 us (96%)
  local copies, waits for them, and re-layouts  2.16 us (2%)
    pallas_call x5, Pallas kernels, call(): pl.pallas_call(kernel, out_shape=outputs, in_specs=specs or [VMEM] * len(...  136 us

profile of v1, /device:TPU:6, one launch (start us, length us, event | category | flops | bytes accessed | tf_op | source)
XLA Modules:
  0.0 138.8 jit_solution(16020238030418035406)
XLA Ops:
  0.0 0.8 compare_select_fusion.4
  0.8 0.6 broadcast_in_dim.11.code_ref
  1.4 39.6 %gather.1 = (f32[32,24,256]{2,1,0:T(8,128)}, f32[16,24,256]{2,1,0:T(8,128)}, bf16[32,32,256]{2,1,0:T(8,128)(2,1)}, bf16[16,32,256]{2,1,0:T(8,128)(2,1)}, s32[32,128]{1,0:T(8,128)}) custom-call(f32[3,16,256]{2,1,0:T(8,128)} %pos_ref.1, f32[2,16,256]{2,1,0:T(8,128)} %facing_ref.1, f32[16,256]{1,0:T(8,128)} %area_ref.3, f32[16,8,256]{2,1,0:T(8,128)} %emission_ref.1, ...), custom_call_target="tpu_custom_call" | custom-call | tf_op jit(solution)/shard_map/gather/pallas_call | solution.py:478
  40.9 20.0 %pairs.1 = (f32[128,8,256]{2,1,0:T(8,128)}, f32[64,8,256]{2,1,0:T(8,128)}, s32[544]{0:T(1024)}, bf16[128,2,256,256]{3,2,1,0:T(8,128)(2,1)}) custom-call(s32[32,128]{1,0:T(8,128)} %get-tuple-element.18.lists_ref, f32[32,24,256]{2,1,0:T(8,128)} %get-tuple-element.19.geo_s, f32[16,24,256]{2,1,0:T(8,128)} %get-tuple-element.20.geo_t, ...), custom_call_target="tpu_custom_call" | custom-call | tf_op jit(solution)/shard_map/pairs/pallas_call | solution.py:478
  60.9 35.7 %turn.1 = (bf16[32,32,256]{2,1,0:T(8,128)(2,1)}, bf16[16,32,256]{2,1,0:T(8,128)(2,1)}) custom-call(f32[32,32,256]{2,1,0:T(8,128)} %bitcast.14, f32[16,32,256]{2,1,0:T(8,128)} %bitcast.16, f32[16,256]{1,0:T(8,128)} %area_ref.3, f32[4,32,256]{2,1,0:T(8,128)} %bitcast.12, f32[4,32,256]{2,1,0:T(8,128)} %bitcast.17), custom_call_target="tpu_custom_call" | custom-call | tf_op jit(solution)/shard_map/turn/pallas_call | solution.py:478
  96.6 10.6 %again.1 = (f32[128,8,256]{2,1,0:T(8,128)}, f32[64,8,256]{2,1,0:T(8,128)}) custom-call(s32[544]{0:T(1024)} %get-tuple-element.23.order, f32[32,24,256]{2,1,0:T(8,128)} %get-tuple-element.19.geo_s, f32[16,24,256]{2,1,0:T(8,128)} %get-tuple-element.20.geo_t, bf16[32,32,256]{2,1,0:T(8,128)(2,1)} %get-tuple-element.26.w_s, ...), custom_call_target="tpu_custom_call" | custom-call | tf_op jit(solution)/shard_map/again/pallas_call | solution.py:478
  107.2 30.0 %last.1 = f32[4,32,256]{2,1,0:T(8,128)} custom-call(f32[32,32,256]{2,1,0:T(8,128)} %bitcast.15, f32[16,32,256]{2,1,0:T(8,128)} %bitcast.19, f32[4,32,256]{2,1,0:T(8,128)} %bitcast.13, f32[4,32,256]{2,1,0:T(8,128)} %bitcast.18), custom_call_target="tpu_custom_call" | custom-call | tf_op jit(solution)/shard_map/last/pallas_call | solution.py:478
  137.2 1.6 %copy.8 = f32[16,8,256]{2,1,0:T(8,128)} copy(f32[16,8,256]{2,1,0:T(8,128)} %bitcast.20) | data formatting | bytes 262144
